TPU v7x, 32 devices: a whole 2x2x4 slice. The times are simulated.
32 devices in a mesh: seq: 16 (over z, y, core), head: 2 (over x).
Axes of the slice: x: 2, y: 2, z: 4, core: 2. Of those that a mesh axis runs over, the one named last changes fastest.
Arguments:
- tokens: bfloat16 [512, 2048], P('seq', 'head'), may hold values from -6 to 6
- ln1_gain: float32 [2048], replicated, may hold values from 0.1 to 1.9
- ln1_shift: float32 [2048], replicated, may hold values from -1.75 to 1.75
- ln2_gain: float32 [2048], replicated, may hold values from 0.1 to 1.9
- ln2_shift: float32 [2048], replicated, may hold values from -1.75 to 1.75
- w_qkv: bfloat16 [2048, 3, 2048], P(None, None, 'head'), may hold values from -0.125 to 0.125
- b_qkv: float32 [3, 2048], P(None, 'head'), may hold values from -3 to 3
- w_dense: bfloat16 [2048, 2048], P('head'), may hold values from -0.125 to 0.125
- b_dense: float32 [2048], P('head'), may hold values from -1.75 to 1.75
- w_up: bfloat16 [2048, 4096], P(None, 'head'), may hold values from -0.125 to 0.125
- b_up: float32 [4096], P('head'), may hold values from -3 to 3
- w_down: bfloat16 [4096, 2048], P('head'), may hold values from -0.09375 to 0.09375
- b_down: float32 [2048], P('head'), may hold values from -1.75 to 1.75
- keys_short: bfloat16 [512, 64, 2048], P('seq', None, 'head'), may hold values from -210 to 210
- values_short: bfloat16 [512, 64, 2048], P('seq', None, 'head'), may hold values from -16 to 16
- keys_long: bfloat16 [32768, 2048], P('seq', 'head'), may hold values from -210 to 210
- values_long: bfloat16 [32768, 2048], P('seq', 'head'), may hold values from -16 to 16
- lengths: int32 [512], replicated, may hold values from 16 to 8192, as said below
- slot_request: int32 [512], replicated, may hold values from 0 to 511, as said below
- piece_map: int32 [16], replicated, may hold values from 0 to 15, each once
Outputs:
- layer_out: bfloat16 [512, 2048], P('seq', 'head')
Inputs may be any that keep to these rules, and one draw needn't show every extreme that they name: `lengths`: requests 0 to 3 hold more than 4096 positions, one of them exactly 8192; every other request holds 16 to 64 positions, one of them exactly 64. `slot_request`: A permutation of the requests; slot s lies on index s // 32 of seq. The requests 32 h to 32 h + 31 are served in 8 groups of exactly 4 on as many different indices of seq. Rows 2048 b to 2048 b + 2047 of keys_long and values_long hold positions (piece_map[b] % 4) * 2048 onwards of the cache of request piece_map[b] // 4.
All inputs are finite; a program needn't handle non-finite values.
Results may differ from a plain program's by a relative error of at most 0.0095.
Values may be sent and summed in bfloat16 or wider, within the bound.
A program may use at most 192 MiB of HBM per device.

v0:
```python
import jax
import jax.numpy as jnp
from jax import lax
from jax.sharding import PartitionSpec as P

HD = 256
ROT = 64
LONGS = 4
epsilon = 1e-05
very_low = -1e30


def merged(array, axis, combine):
    everything = jax.tree.map(lambda part: lax.all_gather(part, axis), array)
    first = jax.tree.map(lambda part: part[0], everything)

    def hop(k, so_far):
        return combine(so_far, jax.tree.map(lambda part: part[k], everything))

    return lax.fori_loop(1, lax.axis_size(axis), hop, first)


def layer_norm(values, gain, shift):
    center = jnp.mean(values, axis=-1, keepdims=True)
    offset = values - center
    spread = jnp.mean(offset * offset, axis=-1, keepdims=True)
    return offset * lax.rsqrt(spread + epsilon) * gain + shift


def rotary(values, position):
    half_rot = ROT // 2
    frequency = jnp.power(10000.0, -2.0 * jnp.arange(half_rot, dtype=jnp.float32) / ROT)
    angles = position.astype(jnp.float32)[:, None] * frequency[None, :]
    cosine = jnp.cos(angles)[:, None, :]
    sine_of = jnp.sin(angles)[:, None, :]
    leading = values[..., :half_rot]
    trailing = values[..., half_rot:ROT]
    return jnp.concatenate(
        [
            leading * cosine - trailing * sine_of,
            trailing * cosine + leading * sine_of,
            values[..., ROT:],
        ],
        axis=-1,
    )


def attend(queries, key_rows, value_rows, usable):
    scores = jnp.einsum(
        "rhc,rthc->rht", queries, key_rows, preferred_element_type=jnp.float32
    ) * HD ** (-0.5)
    masked = jnp.where(usable[:, None, :], scores, very_low)
    summit = jnp.max(masked, axis=-1)
    weights = jnp.where(usable[:, None, :], jnp.exp(masked - summit[..., None]), 0.0)
    amount = jnp.sum(weights, axis=-1)
    mixed = jnp.einsum(
        "rht,rthc->rhc",
        weights.astype(jnp.bfloat16),
        value_rows,
        preferred_element_type=jnp.float32,
    )
    return (summit, amount, mixed)


def combine_partials(first_part, second_part):
    top_first, total_first, out_first = first_part
    top_second, total_second, out_second = second_part
    summit = jnp.maximum(top_first, top_second)
    scale_first = jnp.exp(top_first - summit)
    scale_second = jnp.exp(top_second - summit)
    total_both = total_first * scale_first + total_second * scale_second
    out_both = out_first * scale_first[..., None] + out_second * scale_second[..., None]
    return (summit, total_both, out_both)


def local(
    tokens,
    ln1_gain,
    ln1_shift,
    ln2_gain,
    ln2_shift,
    w_qkv,
    b_qkv,
    w_dense,
    b_dense,
    w_up,
    b_up,
    w_down,
    b_down,
    keys_short,
    values_short,
    keys_long,
    values_long,
    lengths,
    slot_request,
    piece_map,
):
    slot_rows, part_width = tokens.shape
    seq_count = lax.axis_size("seq")
    seq_place = lax.axis_index("seq")
    request_count = slot_request.shape[0]
    heads_here = part_width // HD
    my_requests = lax.dynamic_slice_in_dim(slot_request, seq_place * slot_rows, slot_rows)
    shard_rows = lax.all_gather(tokens, "seq", axis=0, tiled=True)
    row_ids = jnp.arange(shard_rows.shape[0], dtype=jnp.int32)
    selector = (my_requests[:, None] == row_ids[None, :]).astype(jnp.bfloat16)
    own_cols = jnp.dot(selector, shard_rows, preferred_element_type=jnp.float32).astype(
        jnp.bfloat16
    )
    full_rows = lax.all_gather(own_cols, "head", axis=1, tiled=True)
    resident = full_rows.astype(jnp.float32)
    normed_attn = layer_norm(resident, ln1_gain, ln1_shift).astype(jnp.bfloat16)
    normed_mlp = layer_norm(resident, ln2_gain, ln2_shift).astype(jnp.bfloat16)
    projected = jnp.dot(
        normed_attn,
        w_qkv.reshape(w_qkv.shape[0], 3 * part_width),
        preferred_element_type=jnp.float32,
    )
    projected = projected.reshape(slot_rows, 3, part_width) + b_qkv[None]
    request_ids = jnp.arange(request_count, dtype=jnp.int32)
    my_lengths = jnp.sum(
        jnp.where(my_requests[:, None] == request_ids[None, :], lengths[None, :], 0), axis=1
    )
    queries = rotary(projected[:, 0].reshape(slot_rows, heads_here, HD), my_lengths).astype(
        jnp.bfloat16
    )
    new_keys = rotary(projected[:, 1].reshape(slot_rows, heads_here, HD), my_lengths).astype(
        jnp.bfloat16
    )
    new_values = projected[:, 2].reshape(slot_rows, heads_here, HD).astype(jnp.bfloat16)
    long_hits = my_requests[:, None] == jnp.arange(LONGS, dtype=jnp.int32)[None, :]
    long_part = jnp.sum(
        jnp.where(long_hits[:, :, None, None], queries.astype(jnp.float32)[:, None], 0.0), axis=0
    )
    long_queries = lax.psum(long_part, "seq")
    short_max = keys_short.shape[1]
    short_usable = (jnp.arange(short_max, dtype=jnp.int32)[None, :] < my_lengths[:, None]) & (
        my_lengths <= short_max
    )[:, None]
    short_keys = keys_short.reshape(slot_rows, short_max, heads_here, HD)
    short_vals = values_short.reshape(slot_rows, short_max, heads_here, HD)
    short_top, short_total, short_out = attend(queries, short_keys, short_vals, short_usable)
    own_score = jnp.sum(
        queries.astype(jnp.float32) * new_keys.astype(jnp.float32), axis=-1
    ) * HD ** (-0.5)
    piece_count = seq_count // LONGS
    my_piece = lax.dynamic_slice_in_dim(piece_map, seq_place, 1)[0]
    long_owner = my_piece // piece_count
    piece_index = my_piece % piece_count
    long_pick = jnp.arange(LONGS, dtype=jnp.int32) == long_owner
    piece_query = jnp.sum(jnp.where(long_pick[:, None, None], long_queries, 0.0), axis=0).astype(
        jnp.bfloat16
    )
    long_length = jnp.sum(jnp.where(long_pick, lengths[:LONGS], 0))
    piece_len = keys_long.shape[0]
    positions = piece_index * piece_len + jnp.arange(piece_len, dtype=jnp.int32)
    piece_usable = (positions < long_length)[None, :]
    piece_keys = keys_long.reshape(1, piece_len, heads_here, HD)
    piece_vals = values_long.reshape(1, piece_len, heads_here, HD)
    piece_top, piece_total, piece_out = attend(
        piece_query[None], piece_keys, piece_vals, piece_usable
    )
    spread_top = jnp.where(long_pick[:, None], piece_top, very_low)
    spread_total = jnp.where(long_pick[:, None], piece_total, 0.0)
    spread_out = jnp.where(long_pick[:, None, None], piece_out, 0.0)
    long_top, long_total, long_out = merged(
        (spread_top, spread_total, spread_out), "seq", combine_partials
    )
    has_long = jnp.any(long_hits, axis=1)
    mine_top = jnp.where(
        has_long[:, None],
        jnp.sum(jnp.where(long_hits[:, :, None], long_top[None], 0.0), axis=1),
        very_low,
    )
    mine_total = jnp.sum(jnp.where(long_hits[:, :, None], long_total[None], 0.0), axis=1)
    mine_out = jnp.sum(jnp.where(long_hits[:, :, None, None], long_out[None], 0.0), axis=1)
    summit = jnp.maximum(jnp.maximum(short_top, own_score), mine_top)
    short_scale = jnp.exp(short_top - summit)
    own_scale = jnp.exp(own_score - summit)
    long_scale = jnp.exp(mine_top - summit)
    denominator = short_total * short_scale + own_scale + mine_total * long_scale
    numerator = (
        short_out * short_scale[..., None]
        + new_values.astype(jnp.float32) * own_scale[..., None]
        + mine_out * long_scale[..., None]
    )
    attended = (
        (numerator / denominator[..., None]).reshape(slot_rows, part_width).astype(jnp.bfloat16)
    )
    hidden_units = jax.nn.gelu(
        jnp.dot(normed_mlp, w_up, preferred_element_type=jnp.float32) + b_up, approximate=False
    ).astype(jnp.bfloat16)
    partial_sum = jnp.dot(attended, w_dense, preferred_element_type=jnp.float32) + jnp.dot(
        hidden_units, w_down, preferred_element_type=jnp.float32
    )
    head_total = lax.psum_scatter(
        partial_sum.astype(jnp.bfloat16), "head", scatter_dimension=1, tiled=True
    ).astype(jnp.float32)
    finished = (own_cols.astype(jnp.float32) + head_total + b_dense + b_down).astype(jnp.bfloat16)
    home_ids = seq_place * slot_rows + jnp.arange(slot_rows, dtype=jnp.int32)
    selector = (slot_request[None, :] == home_ids[:, None]).astype(jnp.bfloat16)
    return jnp.dot(
        selector,
        lax.all_gather(finished, "seq", axis=0, tiled=True),
        preferred_element_type=jnp.float32,
    ).astype(jnp.bfloat16)


def solution(mesh):
    in_specs = (
        P("seq", "head"),
        P(),
        P(),
        P(),
        P(),
        P(None, None, "head"),
        P(None, "head"),
        P("head", None),
        P("head"),
        P(None, "head"),
        P("head"),
        P("head", None),
        P("head"),
        P("seq", None, "head"),
        P("seq", None, "head"),
        P("seq", "head"),
        P("seq", "head"),
        P(),
        P(),
        P(),
    )
    out_specs = P("seq", "head")
    return jax.shard_map(local, mesh=mesh, in_specs=in_specs, out_specs=out_specs, check_vma=False)
```

profile of v0, /device:TPU:0, one launch (start us, length us, event | category | flops | bytes accessed | tf_op | source)
XLA Modules:
  0.0 262.1 jit_solution(12537288334544157710)
XLA Ops:
  6.5 0.7 all-gather.3.cloned.1.call-update
  7.3 1.2 dynamic_slice.37
  11.2 17.0 %copy.30 = bf16[2048,3,1024]{0,2,1:T(8,128)(2,1)} copy(bf16[2048,3,1024]{2,0,1:T(8,128)(2,1)} %param.27) | data formatting | bytes 25165824 | tf_op args[5]
  28.5 6.5 %copy.47 = bf16[2048,1024]{0,1:T(8,128)(2,1)} copy(bf16[2048,1024]{1,0:T(8,128)(2,1)} %param.37) | data formatting | bytes 8388608 | tf_op jit(solution)/shard_map/reshape.2
  35.0 0.6 select_reduce_fusion.6
  36.5 13.8 %all-gather.3.cloned.1.call-done = bf16[512,1024]{1,0:T(8,128)(2,1)} async-done(((bf16[32,1024]{1,0:T(8,128)(2,1)}), bf16[512,1024]{1,0:T(8,128)(2,1)}) %all-gather.3.cloned.1.call-update) | async-done | bytes 1048592 | tf_op jit(solution)/shard_map/all_gather | solution.py:104
  50.3 1.5 convolution_convert_fusion.1
  51.8 4.9 %all_gather.22 = bf16[32,2048]{1,0:T(8,128)(2,1)S(1)} all-gather(bf16[32,1024]{1,0:T(8,128)(2,1)S(1)} %convolution_convert_fusion.1), channel_id=1, replica_groups=mesh['seq'=16,'head'=2] {'head'}, dimensions={1}, use_global_device_ids=true | all-gather | bytes 196608 | tf_op jit(solution)/shard_map/all_gather | solution.py:110
  57.2 8.5 %fusion.15 = f32[32,3,1024]{2,0,1:T(8,128)S(1)} fusion(bf16[2048,3,1024]{0,2,1:T(8,128)(2,1)} %copy.30, f32[3,1024]{1,0:T(4,128)S(1)} %copy-done.1, bf16[32,2048]{1,0:T(8,128)(2,1)S(1)} %all_gather.22, f32[2048]{0:T(1024)S(1)} %copy-done.5, f32[2048]{0:T(1024)S(1)} %copy-done.6, f32[32]{0:T(128)S(1)} %add_rsqrt_fusion, f32[32]{0:T(128)S(1)} %broadcast_multiply_fusion), kind=kOutput, calls=%fused_computation.22 | convolution fusion | flops 403144704 | bytes 13136128 | tf_op jit(solution)/shard_map/dot_general | solution.py:114
  66.6 3.4 %fusion.11 = f32[32,4,1,64]{3,2,1,0:T(1,128)S(1)} fusion(bf16[32,8,4,8,256]{4,3,2,1,0:T(8,128)(2,1)} %bitcast.118, bf16[32,4,256,1]{2,1,0,3:T(4,128)(2,1)S(1)} %bitcast.115), kind=kOutput, calls=%fused_computation.16 | convolution fusion | flops 4194304 | bytes 4292608 | tf_op jit(solution)/shard_map/rhc,rthc->rht/dot_general | solution.py:49
  70.4 58.4 %psum.7 = f32[4,4,256]{2,1,0:T(4,128)S(1)} all-reduce(f32[4,4,256]{2,1,0:T(4,128)S(1)} %select_reduce_fusion.1), channel_id=1, replica_groups=mesh['seq'=16,'head'=2] {'seq'}, use_global_device_ids=true, to_apply=%region_8.9 | all-reduce | flops 4096 | bytes 32768 | tf_op jit(solution)/shard_map/psum | solution.py:135
  128.9 3.0 %fusion.108 = f32[4,1,2048]{2,1,0:T(1,128)S(1)} fusion(bf16[2048,4,256]{0,2,1:T(8,128)(2,1)} %bitcast.112, bf16[4,256,1]{1,0,2:T(4,128)(2,1)S(1)} %bitcast.116), kind=kOutput, calls=%fused_computation.149 | convolution fusion | flops 4194304 | bytes 4229120 | tf_op jit(solution)/shard_map/rhc,rthc->rht/dot_general | solution.py:49
  132.3 0.7 fusion.5
  133.0 17.8 %all_gather.25 = f32[16,4,4,256]{3,2,1,0:T(4,128)S(1)} all-gather(f32[1,4,4,256]{3,2,1,0:T(4,128)S(1)} %broadcast_select_fusion), channel_id=1, replica_groups=mesh['seq'=16,'head'=2] {'seq'}, dimensions={0}, use_global_device_ids=true | all-gather | bytes 278528 | tf_op jit(solution)/shard_map/all_gather | solution.py:14
  150.9 19.3 %all_gather.24 = f32[16,4,4]{2,1,0:T(4,128)S(1)} all-gather(f32[1,4,4]{2,1,0:T(4,128)S(1)} %get-tuple-element.228), channel_id=1, replica_groups=mesh['seq'=16,'head'=2] {'seq'}, dimensions={0}, use_global_device_ids=true | all-gather | bytes 1088 | tf_op jit(solution)/shard_map/all_gather | solution.py:14
  170.2 17.7 %all_gather.23 = f32[16,4,4]{2,1,0:T(4,128)S(1)} all-gather(f32[1,4,4]{2,1,0:T(4,128)S(1)} %get-tuple-element.229), channel_id=1, replica_groups=mesh['seq'=16,'head'=2] {'seq'}, dimensions={0}, use_global_device_ids=true | all-gather | bytes 1088 | tf_op jit(solution)/shard_map/all_gather | solution.py:14
  187.9 2.0 while.19
  190.1 3.0 %fusion.8 = f32[32,4,1,256]{3,2,1,0:T(1,128)S(1)} fusion(bf16[32,8,4,8,256]{4,3,2,1,0:T(8,128)(2,1)} %bitcast.113, bf16[32,4,64,1]{2,0,1,3:T(8,128)(2,1)S(1)} %get-tuple-element.218), kind=kOutput, calls=%fused_computation.13 | convolution fusion | flops 4194304 | bytes 4341760 | tf_op jit(solution)/shard_map/rht,rthc->rhc/dot_general | solution.py:56
  193.5 0.8 fusion.143
  194.4 10.0 %fusion.14 = bf16[32,2048]{1,0:T(8,128)(2,1)} fusion(f32[32,2048]{1,0:T(8,128)S(1)} %fusion.143, bf16[2048,2048]{1,0:T(8,128)(2,1)} %param.33, bf16[2048,2048]{1,0:T(8,128)(2,1)} %param.31, bf16[32,2048]{1,0:T(8,128)(2,1)S(1)} %all_gather.22, f32[2048]{0:T(1024)S(1)} %copy-done.2, f32[2048]{0:T(1024)S(1)} %copy-done.3, f32[2048]{0:T(1024)S(1)} %copy-done.4, ...), kind=kOutput, calls=%fused_computation.21 | convolution fusion | flops 541720576 | bytes 17326336 | tf_op jit(solution)/shard_map/dot_general | solution.py:193
  204.5 8.8 %reduce-scatter.2.cloned.1.call-done = bf16[32,1024]{1,0:T(8,128)(2,1)} async-done(((bf16[32,2048]{1,0:T(8,128)(2,1)}), bf16[32,1024]{1,0:T(8,128)(2,1)}) %reduce-scatter.2.cloned.1.call-update) | async-done | bytes 65552 | tf_op jit(solution)/shard_map/reduce_scatter | solution.py:196
  213.2 1.5 add_convert_fusion
  214.8 38.6 %all-gather.5.cloned.1.call-done = bf16[512,1024]{1,0:T(8,128)(2,1)} async-done(((bf16[32,1024]{1,0:T(8,128)(2,1)}), bf16[512,1024]{1,0:T(8,128)(2,1)}) %all-gather.5.cloned.1.call-update) | async-done | bytes 1048592 | tf_op jit(solution)/shard_map/all_gather | solution.py:204
  253.4 2.2 convolution_convert_fusion
  (102 shorter events, 5.9 us)
Async XLA Ops:
  6.5 43.8 %all-gather.3.cloned.1.call-start = ((), (), s32[]{:S(2)}) async-start(), calls=%async_computation.1 | async-start | bytes 1114112 | tf_op jit(solution)/shard_map/all_gather | solution.py:104
  7.3 206.0 %reduce-scatter.2.cloned.1.call-start = ((), (), s32[]{:S(2)}) async-start(), calls=%async_computation.2 | async-start | bytes 196608 | tf_op jit(solution)/shard_map/reduce_scatter | solution.py:196
  11.2 17.0 %copy-start.9 = (s32[512]{0:T(512)S(1)}, s32[512]{0:T(512)}, u32[]{:S(2)}) copy-start(s32[512]{0:T(512)} %param.40) | copy-start | bytes 6148
  11.2 17.1 %copy-start.10 = (s32[512]{0:T(512)S(1)}, s32[512]{0:T(512)}, u32[]{:S(2)}) copy-start(s32[512]{0:T(512)} %param.39) | copy-start | bytes 6148
  28.4 28.7 %copy-start.1 = (f32[3,1024]{1,0:T(4,128)S(1)}, f32[3,1024]{1,0:T(4,128)}, u32[]{:S(2)}) copy-start(f32[3,1024]{1,0:T(4,128)} %param.28) | copy-start | bytes 36868
  28.4 28.7 %copy-start.5 = (f32[2048]{0:T(1024)S(1)}, f32[2048]{0:T(1024)}, u32[]{:S(2)}) copy-start(f32[2048]{0:T(1024)} %param.24) | copy-start | bytes 24580
  28.5 28.7 %copy-start.6 = (f32[2048]{0:T(1024)S(1)}, f32[2048]{0:T(1024)}, u32[]{:S(2)}) copy-start(f32[2048]{0:T(1024)} %param.23) | copy-start | bytes 24580
  128.8 3.4 %copy-start.11 = (bf16[2048,1024]{1,0:T(8,128)(2,1)S(1)}, bf16[2048,1024]{1,0:T(8,128)(2,1)}, u32[]{:S(2)}) copy-start(bf16[2048,1024]{1,0:T(8,128)(2,1)} %param.38) | copy-start | bytes 12582916
  190.1 3.5 %copy-start = (bf16[1024,2048]{1,0:T(8,128)(2,1)S(1)}, bf16[1024,2048]{1,0:T(8,128)(2,1)}, u32[]{:S(2)}) copy-start(bf16[1024,2048]{1,0:T(8,128)(2,1)} %param.29) | copy-start | bytes 12582916
  190.1 4.3 %copy-start.2 = (f32[2048]{0:T(1024)S(1)}, f32[2048]{0:T(1024)}, u32[]{:S(2)}) copy-start(f32[2048]{0:T(1024)} %param.32) | copy-start | bytes 24580
  190.1 4.3 %copy-start.3 = (f32[2048]{0:T(1024)S(1)}, f32[2048]{0:T(1024)}, u32[]{:S(2)}) copy-start(f32[2048]{0:T(1024)} %param.26) | copy-start | bytes 24580
  190.1 4.3 %copy-start.4 = (f32[2048]{0:T(1024)S(1)}, f32[2048]{0:T(1024)}, u32[]{:S(2)}) copy-start(f32[2048]{0:T(1024)} %param.25) | copy-start | bytes 24580
  194.4 18.9 %copy-start.7 = (f32[1024]{0:T(1024)S(1)}, f32[1024]{0:T(1024)}, u32[]{:S(2)}) copy-start(f32[1024]{0:T(1024)} %param.34) | copy-start | bytes 12292
  194.4 18.8 %copy-start.8 = (f32[1024]{0:T(1024)S(1)}, f32[1024]{0:T(1024)}, u32[]{:S(2)}) copy-start(f32[1024]{0:T(1024)} %param.30) | copy-start | bytes 12292
  204.4 49.0 %all-gather.5.cloned.1.call-start = ((), (), s32[]{:S(2)}) async-start(), calls=%async_computation.3 | async-start | bytes 1114112 | tf_op jit(solution)/shard_map/all_gather | solution.py:204
Sparse Core Ops, SparseCore 0:
  9.5 40.7 all-gather.2
  204.5 8.6 reduce-scatter.1
  215.4 37.9 all-gather.4
where the time goes:
time: 263 us; the launch traced here: 262 us
  blocking collectives  118 us (45%)
  waiting for transfers between devices  61.9 us (24%)
  matrix products  33 us (13%)
  local copies, waits for them, and re-layouts  25.6 us (10%)
  between operations  16 us (6%)
  other arithmetic  7.06 us (3%)
    psum x1, blocking collectives, local(): long_queries = lax.psum(long_part, 'seq')  58.4 us
    all_gather x3, blocking collectives, merged(): everything = jax.tree.map(lambda part: lax.all_gather(part, axis), array)  54.8 us
    all_gather x1, waiting for transfers between devices, local(): lax.all_gather(finished, 'seq', axis=0, tiled=True)  38.6 us
    unnamed x25, local copies, waits for them, and re-layouts  17.2 us
    all_gather x1, waiting for transfers between devices, local(): shard_rows = lax.all_gather(tokens, 'seq', axis=0, tiled=True)  13.8 us
    dot_general x1, matrix products, local(): jnp.dot(hidden_units, w_down, preferred_element_type=jnp.float32)  9.99 us
    reduce_scatter x1, waiting for transfers between devices, local(): lax.psum_scatter(partial_sum.astype(jnp.bfloat16), 'head', scatter_dimens...  8.76 us
    dot_general x1, matrix products, local(): jnp.dot(normed_attn, w_qkv.reshape(w_qkv.shape[0], 3 * part_width), prefe...  8.47 us
  transfers between devices with their start and end apart: 3, of which 3 were waited for; matrix products, arithmetic and copies ran while one was open for 10% of the time, Pallas kernels for 0%

commit v1 on v0

--- a/solution.py
+++ b/solution.py
@@ -8,6 +8,27 @@
 LONGS = 4
 epsilon = 1e-05
 very_low = -1e30
+
+
+def gather_around(x, axis, dim):
+    count, index, rows = (lax.axis_size(axis), lax.axis_index(axis), x.shape[dim])
+    right = [(i, (i + 1) % count) for i in range(count)]
+    backward = [(i, (i - 1) % count) for i in range(count)]
+    out = jnp.zeros((*x.shape[:dim], count * rows, *x.shape[dim + 1 :]), x.dtype)
+    out = lax.dynamic_update_slice_in_dim(out, x, index * rows, axis=dim)
+    from_left = from_right = x
+    half = count // 2
+    for turn in range(1, half + 1):
+        from_left = lax.ppermute(from_left, axis, right)
+        out = lax.dynamic_update_slice_in_dim(
+            out, from_left, (index - turn) % count * rows, axis=dim
+        )
+        if turn < count - half:
+            from_right = lax.ppermute(from_right, axis, backward)
+            out = lax.dynamic_update_slice_in_dim(
+                out, from_right, (index + turn) % count * rows, axis=dim
+            )
+    return out
 
 
 def merged(array, axis, combine):
@@ -101,7 +122,7 @@
     request_count = slot_request.shape[0]
     heads_here = part_width // HD
     my_requests = lax.dynamic_slice_in_dim(slot_request, seq_place * slot_rows, slot_rows)
-    shard_rows = lax.all_gather(tokens, "seq", axis=0, tiled=True)
+    shard_rows = gather_around(tokens, "seq", 0)
     row_ids = jnp.arange(shard_rows.shape[0], dtype=jnp.int32)
     selector = (my_requests[:, None] == row_ids[None, :]).astype(jnp.bfloat16)
     own_cols = jnp.dot(selector, shard_rows, preferred_element_type=jnp.float32).astype(

time: 263 us -> 301 us (1.14)
  starting transfers between devices: 0.08 us -> 32.4 us
  waiting for transfers between devices: 61.9 us -> 65.6 us
    ppermute x0 -> x15, starting transfers between devices: none -> 32.3 us  [the longest x7 31.8 us: gather_around(): from_right = lax.ppermute(from_right, axis, backward)]
    ppermute x0 -> x15, waiting for transfers between devices: none -> 17.7 us  [the longest x8 17.6 us: gather_around(): from_left = lax.ppermute(from_left, axis, right)]
    all_gather x1 -> x0, waiting for transfers between devices: 13.8 us -> none  [local(): shard_rows = lax.all_gather(tokens, 'seq', axis=0, tiled=True)]
    unnamed x25 -> x23, local copies, waits for them, and re-layouts: 17.2 us -> 17.2 us
  transfers between devices with their start and end apart: 3 -> 17, of which waited for: 3 -> 9; matrix products, arithmetic and copies ran while one was open for 10% -> 10% of each run, Pallas kernels for 0% -> 0%
where the time goes in v1:
time: 301 us; the launch traced here: 300 us
  blocking collectives  117 us (39%)
  waiting for transfers between devices  65.6 us (22%)
  starting transfers between devices  32.4 us (11%)
  matrix products  31.8 us (11%)
  local copies, waits for them, and re-layouts  27.4 us (9%)
  between operations  16.4 us (5%)
  other arithmetic  8.44 us (3%)
    psum x1, blocking collectives, local(): long_queries = lax.psum(long_part, 'seq')  57.6 us
    all_gather x3, blocking collectives, merged(): everything = jax.tree.map(lambda part: lax.all_gather(part, axis), array)  54.8 us
    all_gather x1, waiting for transfers between devices, local(): lax.all_gather(finished, 'seq', axis=0, tiled=True)  38.6 us
    ppermute x7, starting transfers between devices, gather_around(): from_right = lax.ppermute(from_right, axis, backward)  31.8 us
    ppermute x8, waiting for transfers between devices, gather_around(): from_left = lax.ppermute(from_left, axis, right)  17.6 us
    unnamed x23, local copies, waits for them, and re-layouts  17.2 us
    dot_general x1, matrix products, local(): jnp.dot(hidden_units, w_down, preferred_element_type=jnp.float32)  9.99 us
    reduce_scatter x1, waiting for transfers between devices, local(): lax.psum_scatter(partial_sum.astype(jnp.bfloat16), 'head', scatter_dimens...  9.23 us
  transfers between devices with their start and end apart: 17, of which 9 were waited for; matrix products, arithmetic and copies ran while one was open for 10% of the time, Pallas kernels for 0%

profile of v1, /device:TPU:0, one launch (start us, length us, event | category | flops | bytes accessed | tf_op | source)
XLA Modules:
  0.0 299.5 jit_solution(9034793276446551878)
XLA Ops:
  7.0 5.0 %collective-permute-start.1 = (bf16[32,1024]{1,0:T(8,128)(2,1)}, bf16[32,1024]{1,0:T(8,128)(2,1)S(1)}, u32[]{:S(2)}, u32[]{:S(2)}) collective-permute-start(bf16[32,1024]{1,0:T(8,128)(2,1)} %param.22), channel_id=1, source_target_pairs={{0,30},{2,0},{4,2},{6,4},{8,6},{10,8},{12,10},{14,12},{16,14},{18,... | collective-permute-start | bytes 196616 | tf_op jit(solution)/shard_map/ppermute | solution.py:27
  18.5 17.0 %copy.30 = bf16[2048,3,1024]{0,2,1:T(8,128)(2,1)} copy(bf16[2048,3,1024]{2,0,1:T(8,128)(2,1)} %param.27) | data formatting | bytes 25165824 | tf_op args[5]
  35.5 6.5 %copy.47 = bf16[2048,1024]{0,1:T(8,128)(2,1)} copy(bf16[2048,1024]{1,0:T(8,128)(2,1)} %param.37) | data formatting | bytes 8388608 | tf_op jit(solution)/shard_map/reshape.2
  44.2 4.4 %collective-permute-start.3 = (bf16[32,1024]{1,0:T(8,128)(2,1)S(1)}, bf16[32,1024]{1,0:T(8,128)(2,1)S(1)}, u32[]{:S(2)}, u32[]{:S(2)}) collective-permute-start(bf16[32,1024]{1,0:T(8,128)(2,1)S(1)} %collective-permute-done.1), channel_id=1, source_target_pairs={{0,30},{2,0},{4,2},{6,4},{8,6},{10,8},{12,10},{14,12},{16,14},{18,... | collective-permute-start | bytes 196616 | tf_op jit(solution)/shard_map/ppermute | solution.py:27
  50.6 4.4 %collective-permute-start.5 = (bf16[32,1024]{1,0:T(8,128)(2,1)S(1)}, bf16[32,1024]{1,0:T(8,128)(2,1)S(1)}, u32[]{:S(2)}, u32[]{:S(2)}) collective-permute-start(bf16[32,1024]{1,0:T(8,128)(2,1)S(1)} %collective-permute-done.3), channel_id=1, source_target_pairs={{0,30},{2,0},{4,2},{6,4},{8,6},{10,8},{12,10},{14,12},{16,14},{18,... | collective-permute-start | bytes 196616 | tf_op jit(solution)/shard_map/ppermute | solution.py:27
  57.0 4.5 %collective-permute-start.7 = (bf16[32,1024]{1,0:T(8,128)(2,1)S(1)}, bf16[32,1024]{1,0:T(8,128)(2,1)S(1)}, u32[]{:S(2)}, u32[]{:S(2)}) collective-permute-start(bf16[32,1024]{1,0:T(8,128)(2,1)S(1)} %collective-permute-done.5), channel_id=1, source_target_pairs={{0,30},{2,0},{4,2},{6,4},{8,6},{10,8},{12,10},{14,12},{16,14},{18,... | collective-permute-start | bytes 196616 | tf_op jit(solution)/shard_map/ppermute | solution.py:27
  63.4 4.5 %collective-permute-start.9 = (bf16[32,1024]{1,0:T(8,128)(2,1)S(1)}, bf16[32,1024]{1,0:T(8,128)(2,1)S(1)}, u32[]{:S(2)}, u32[]{:S(2)}) collective-permute-start(bf16[32,1024]{1,0:T(8,128)(2,1)S(1)} %collective-permute-done.7), channel_id=1, source_target_pairs={{0,30},{2,0},{4,2},{6,4},{8,6},{10,8},{12,10},{14,12},{16,14},{18,... | collective-permute-start | bytes 196616 | tf_op jit(solution)/shard_map/ppermute | solution.py:27
  69.8 4.5 %collective-permute-start.11 = (bf16[32,1024]{1,0:T(8,128)(2,1)S(1)}, bf16[32,1024]{1,0:T(8,128)(2,1)S(1)}, u32[]{:S(2)}, u32[]{:S(2)}) collective-permute-start(bf16[32,1024]{1,0:T(8,128)(2,1)S(1)} %collective-permute-done.9), channel_id=1, source_target_pairs={{0,30},{2,0},{4,2},{6,4},{8,6},{10,8},{12,10},{14,12},{16,14},{18,... | collective-permute-start | bytes 196616 | tf_op jit(solution)/shard_map/ppermute | solution.py:27
  76.2 4.5 %collective-permute-start.13 = (bf16[32,1024]{1,0:T(8,128)(2,1)S(1)}, bf16[32,1024]{1,0:T(8,128)(2,1)S(1)}, u32[]{:S(2)}, u32[]{:S(2)}) collective-permute-start(bf16[32,1024]{1,0:T(8,128)(2,1)S(1)} %collective-permute-done.11), channel_id=1, source_target_pairs={{0,30},{2,0},{4,2},{6,4},{8,6},{10,8},{12,10},{14,12},{16,14},{18,... | collective-permute-start | bytes 196616 | tf_op jit(solution)/shard_map/ppermute | solution.py:27
  82.6 6.3 %collective-permute-done.14 = bf16[32,1024]{1,0:T(8,128)(2,1)S(1)} collective-permute-done((bf16[32,1024]{1,0:T(8,128)(2,1)S(1)}, bf16[32,1024]{1,0:T(8,128)(2,1)S(1)}, u32[]{:S(2)}, u32[]{:S(2)}) %collective-permute-start.14) | collective-permute-done | bytes 65568 | tf_op jit(solution)/shard_map/ppermute | solution.py:22
  89.2 4.9 %all_gather.18 = bf16[32,2048]{1,0:T(8,128)(2,1)S(1)} all-gather(bf16[32,1024]{1,0:T(8,128)(2,1)S(1)} %convolution_convert_fusion.1), channel_id=1, replica_groups=mesh['seq'=16,'head'=2] {'head'}, dimensions={1}, use_global_device_ids=true | all-gather | bytes 196608 | tf_op jit(solution)/shard_map/all_gather | solution.py:131
  94.6 8.5 %fusion.15 = f32[32,3,1024]{2,0,1:T(8,128)S(1)} fusion(bf16[2048,3,1024]{0,2,1:T(8,128)(2,1)} %copy.30, f32[3,1024]{1,0:T(4,128)S(1)} %copy-done.1, bf16[32,2048]{1,0:T(8,128)(2,1)S(1)} %all_gather.18, f32[2048]{0:T(1024)S(1)} %copy-done.5, f32[2048]{0:T(1024)S(1)} %copy-done.6, f32[32]{0:T(128)S(1)} %add_rsqrt_fusion, f32[32]{0:T(128)S(1)} %broadcast_multiply_fusion), kind=kOutput, calls=%fused_computation.22 | convolution fusion | flops 403144704 | bytes 13136128 | tf_op jit(solution)/shard_map/dot_general | solution.py:135
  104.0 3.4 %fusion.11 = f32[32,4,1,64]{3,2,1,0:T(1,128)S(1)} fusion(bf16[32,8,4,8,256]{4,3,2,1,0:T(8,128)(2,1)} %bitcast.118, bf16[32,4,256,1]{2,1,0,3:T(4,128)(2,1)S(1)} %bitcast.115), kind=kOutput, calls=%fused_computation.16 | convolution fusion | flops 4194304 | bytes 4292608 | tf_op jit(solution)/shard_map/rhc,rthc->rht/dot_general | solution.py:70
  107.8 57.6 %psum.7 = f32[4,4,256]{2,1,0:T(4,128)S(1)} all-reduce(f32[4,4,256]{2,1,0:T(4,128)S(1)} %select_reduce_fusion.1), channel_id=1, replica_groups=mesh['seq'=16,'head'=2] {'seq'}, use_global_device_ids=true, to_apply=%region_8.9 | all-reduce | flops 4096 | bytes 32768 | tf_op jit(solution)/shard_map/psum | solution.py:156
  165.5 3.0 fusion.108
  169.6 17.8 %all_gather.21 = f32[16,4,4,256]{3,2,1,0:T(4,128)S(1)} all-gather(f32[1,4,4,256]{3,2,1,0:T(4,128)S(1)} %broadcast_select_fusion), channel_id=1, replica_groups=mesh['seq'=16,'head'=2] {'seq'}, dimensions={0}, use_global_device_ids=true | all-gather | bytes 278528 | tf_op jit(solution)/shard_map/all_gather | solution.py:35
  187.5 19.3 %all_gather.20 = f32[16,4,4]{2,1,0:T(4,128)S(1)} all-gather(f32[1,4,4]{2,1,0:T(4,128)S(1)} %get-tuple-element.228), channel_id=1, replica_groups=mesh['seq'=16,'head'=2] {'seq'}, dimensions={0}, use_global_device_ids=true | all-gather | bytes 1088 | tf_op jit(solution)/shard_map/all_gather | solution.py:35
  206.8 17.7 %all_gather.19 = f32[16,4,4]{2,1,0:T(4,128)S(1)} all-gather(f32[1,4,4]{2,1,0:T(4,128)S(1)} %get-tuple-element.229), channel_id=1, replica_groups=mesh['seq'=16,'head'=2] {'seq'}, dimensions={0}, use_global_device_ids=true | all-gather | bytes 1088 | tf_op jit(solution)/shard_map/all_gather | solution.py:35
  224.4 2.0 while.19
  226.7 3.0 %fusion.8 = f32[32,4,1,256]{3,2,1,0:T(1,128)S(1)} fusion(bf16[32,8,4,8,256]{4,3,2,1,0:T(8,128)(2,1)} %bitcast.113, bf16[32,4,64,1]{2,0,1,3:T(8,128)(2,1)S(1)} %get-tuple-element.218), kind=kOutput, calls=%fused_computation.13 | convolution fusion | flops 4194304 | bytes 4341760 | tf_op jit(solution)/shard_map/rht,rthc->rhc/dot_general | solution.py:77
  231.0 10.0 %fusion.14 = bf16[32,2048]{1,0:T(8,128)(2,1)} fusion(f32[32,2048]{1,0:T(8,128)S(1)} %fusion.143, bf16[2048,2048]{1,0:T(8,128)(2,1)} %param.33, bf16[2048,2048]{1,0:T(8,128)(2,1)} %param.31, bf16[32,2048]{1,0:T(8,128)(2,1)S(1)} %all_gather.18, f32[2048]{0:T(1024)S(1)} %copy-done.2, f32[2048]{0:T(1024)S(1)} %copy-done.3, f32[2048]{0:T(1024)S(1)} %copy-done.4, ...), kind=kOutput, calls=%fused_computation.21 | convolution fusion | flops 541720576 | bytes 17326336 | tf_op jit(solution)/shard_map/dot_general | solution.py:214
  241.1 9.2 %reduce-scatter.2.cloned.1.call-done = bf16[32,1024]{1,0:T(8,128)(2,1)} async-done(((bf16[32,2048]{1,0:T(8,128)(2,1)}), bf16[32,1024]{1,0:T(8,128)(2,1)}) %reduce-scatter.2.cloned.1.call-update) | async-done | bytes 65552 | tf_op jit(solution)/shard_map/reduce_scatter | solution.py:217
  251.9 38.6 %all-gather.2.cloned.1.call-done = bf16[512,1024]{1,0:T(8,128)(2,1)} async-done(((bf16[32,1024]{1,0:T(8,128)(2,1)}), bf16[512,1024]{1,0:T(8,128)(2,1)}) %all-gather.2.cloned.1.call-update) | async-done | bytes 1048592 | tf_op jit(solution)/shard_map/all_gather | solution.py:225
  290.5 2.2 convolution_convert_fusion
  (144 shorter events, 26.0 us)
Async XLA Ops:
  6.5 243.8 %reduce-scatter.2.cloned.1.call-start = ((), (), s32[]{:S(2)}) async-start(), calls=%async_computation.1 | async-start | bytes 196608 | tf_op jit(solution)/shard_map/reduce_scatter | solution.py:217
  6.5 37.6 %collective-permute-start = (bf16[32,1024]{1,0:T(8,128)(2,1)}, bf16[32,1024]{1,0:T(8,128)(2,1)S(1)}, u32[]{:S(2)}, u32[]{:S(2)}) collective-permute-start(bf16[32,1024]{1,0:T(8,128)(2,1)} %param.22), channel_id=1, source_target_pairs={{0,2},{2,4},{4,6},{6,8},{8,10},{10,12},{12,14},{14,16},{16,18},{18... | collective-permute-start | bytes 196616 | tf_op jit(solution)/shard_map/ppermute | solution.py:22
  7.0 37.2 %collective-permute-start.1 = (bf16[32,1024]{1,0:T(8,128)(2,1)}, bf16[32,1024]{1,0:T(8,128)(2,1)S(1)}, u32[]{:S(2)}, u32[]{:S(2)}) collective-permute-start(bf16[32,1024]{1,0:T(8,128)(2,1)} %param.22), channel_id=1, source_target_pairs={{0,30},{2,0},{4,2},{6,4},{8,6},{10,8},{12,10},{14,12},{16,14},{18,... | collective-permute-start | bytes 196616 | tf_op jit(solution)/shard_map/ppermute | solution.py:27
  35.5 59.0 %copy-start.1 = (f32[3,1024]{1,0:T(4,128)S(1)}, f32[3,1024]{1,0:T(4,128)}, u32[]{:S(2)}) copy-start(f32[3,1024]{1,0:T(4,128)} %param.28) | copy-start | bytes 36868
  35.5 59.0 %copy-start.5 = (f32[2048]{0:T(1024)S(1)}, f32[2048]{0:T(1024)}, u32[]{:S(2)}) copy-start(f32[2048]{0:T(1024)} %param.24) | copy-start | bytes 24580
  35.5 59.1 %copy-start.6 = (f32[2048]{0:T(1024)S(1)}, f32[2048]{0:T(1024)}, u32[]{:S(2)}) copy-start(f32[2048]{0:T(1024)} %param.23) | copy-start | bytes 24580
  44.1 6.5 %collective-permute-start.2 = (bf16[32,1024]{1,0:T(8,128)(2,1)S(1)}, bf16[32,1024]{1,0:T(8,128)(2,1)S(1)}, u32[]{:S(2)}, u32[]{:S(2)}) collective-permute-start(bf16[32,1024]{1,0:T(8,128)(2,1)S(1)} %collective-permute-done), channel_id=1, source_target_pairs={{0,2},{2,4},{4,6},{6,8},{8,10},{10,12},{12,14},{14,16},{16,18},{18... | collective-permute-start | bytes 196616 | tf_op jit(solution)/shard_map/ppermute | solution.py:22
  44.2 6.4 %collective-permute-start.3 = (bf16[32,1024]{1,0:T(8,128)(2,1)S(1)}, bf16[32,1024]{1,0:T(8,128)(2,1)S(1)}, u32[]{:S(2)}, u32[]{:S(2)}) collective-permute-start(bf16[32,1024]{1,0:T(8,128)(2,1)S(1)} %collective-permute-done.1), channel_id=1, source_target_pairs={{0,30},{2,0},{4,2},{6,4},{8,6},{10,8},{12,10},{14,12},{16,14},{18,... | collective-permute-start | bytes 196616 | tf_op jit(solution)/shard_map/ppermute | solution.py:27
  50.6 6.4 %collective-permute-start.4 = (bf16[32,1024]{1,0:T(8,128)(2,1)S(1)}, bf16[32,1024]{1,0:T(8,128)(2,1)S(1)}, u32[]{:S(2)}, u32[]{:S(2)}) collective-permute-start(bf16[32,1024]{1,0:T(8,128)(2,1)S(1)} %collective-permute-done.2), channel_id=1, source_target_pairs={{0,2},{2,4},{4,6},{6,8},{8,10},{10,12},{12,14},{14,16},{16,18},{18... | collective-permute-start | bytes 196616 | tf_op jit(solution)/shard_map/ppermute | solution.py:22
  50.6 6.4 %collective-permute-start.5 = (bf16[32,1024]{1,0:T(8,128)(2,1)S(1)}, bf16[32,1024]{1,0:T(8,128)(2,1)S(1)}, u32[]{:S(2)}, u32[]{:S(2)}) collective-permute-start(bf16[32,1024]{1,0:T(8,128)(2,1)S(1)} %collective-permute-done.3), channel_id=1, source_target_pairs={{0,30},{2,0},{4,2},{6,4},{8,6},{10,8},{12,10},{14,12},{16,14},{18,... | collective-permute-start | bytes 196616 | tf_op jit(solution)/shard_map/ppermute | solution.py:27
  57.0 6.4 %collective-permute-start.6 = (bf16[32,1024]{1,0:T(8,128)(2,1)S(1)}, bf16[32,1024]{1,0:T(8,128)(2,1)S(1)}, u32[]{:S(2)}, u32[]{:S(2)}) collective-permute-start(bf16[32,1024]{1,0:T(8,128)(2,1)S(1)} %collective-permute-done.4), channel_id=1, source_target_pairs={{0,2},{2,4},{4,6},{6,8},{8,10},{10,12},{12,14},{14,16},{16,18},{18... | collective-permute-start | bytes 196616 | tf_op jit(solution)/shard_map/ppermute | solution.py:22
  57.0 6.4 %collective-permute-start.7 = (bf16[32,1024]{1,0:T(8,128)(2,1)S(1)}, bf16[32,1024]{1,0:T(8,128)(2,1)S(1)}, u32[]{:S(2)}, u32[]{:S(2)}) collective-permute-start(bf16[32,1024]{1,0:T(8,128)(2,1)S(1)} %collective-permute-done.5), channel_id=1, source_target_pairs={{0,30},{2,0},{4,2},{6,4},{8,6},{10,8},{12,10},{14,12},{16,14},{18,... | collective-permute-start | bytes 196616 | tf_op jit(solution)/shard_map/ppermute | solution.py:27
  63.4 6.4 %collective-permute-start.8 = (bf16[32,1024]{1,0:T(8,128)(2,1)S(1)}, bf16[32,1024]{1,0:T(8,128)(2,1)S(1)}, u32[]{:S(2)}, u32[]{:S(2)}) collective-permute-start(bf16[32,1024]{1,0:T(8,128)(2,1)S(1)} %collective-permute-done.6), channel_id=1, source_target_pairs={{0,2},{2,4},{4,6},{6,8},{8,10},{10,12},{12,14},{14,16},{16,18},{18... | collective-permute-start | bytes 196616 | tf_op jit(solution)/shard_map/ppermute | solution.py:22
  63.4 6.4 %collective-permute-start.9 = (bf16[32,1024]{1,0:T(8,128)(2,1)S(1)}, bf16[32,1024]{1,0:T(8,128)(2,1)S(1)}, u32[]{:S(2)}, u32[]{:S(2)}) collective-permute-start(bf16[32,1024]{1,0:T(8,128)(2,1)S(1)} %collective-permute-done.7), channel_id=1, source_target_pairs={{0,30},{2,0},{4,2},{6,4},{8,6},{10,8},{12,10},{14,12},{16,14},{18,... | collective-permute-start | bytes 196616 | tf_op jit(solution)/shard_map/ppermute | solution.py:27
  69.8 6.4 %collective-permute-start.10 = (bf16[32,1024]{1,0:T(8,128)(2,1)S(1)}, bf16[32,1024]{1,0:T(8,128)(2,1)S(1)}, u32[]{:S(2)}, u32[]{:S(2)}) collective-permute-start(bf16[32,1024]{1,0:T(8,128)(2,1)S(1)} %collective-permute-done.8), channel_id=1, source_target_pairs={{0,2},{2,4},{4,6},{6,8},{8,10},{10,12},{12,14},{14,16},{16,18},{18... | collective-permute-start | bytes 196616 | tf_op jit(solution)/shard_map/ppermute | solution.py:22
  69.8 6.4 %collective-permute-start.11 = (bf16[32,1024]{1,0:T(8,128)(2,1)S(1)}, bf16[32,1024]{1,0:T(8,128)(2,1)S(1)}, u32[]{:S(2)}, u32[]{:S(2)}) collective-permute-start(bf16[32,1024]{1,0:T(8,128)(2,1)S(1)} %collective-permute-done.9), channel_id=1, source_target_pairs={{0,30},{2,0},{4,2},{6,4},{8,6},{10,8},{12,10},{14,12},{16,14},{18,... | collective-permute-start | bytes 196616 | tf_op jit(solution)/shard_map/ppermute | solution.py:27
  76.1 6.4 %collective-permute-start.12 = (bf16[32,1024]{1,0:T(8,128)(2,1)S(1)}, bf16[32,1024]{1,0:T(8,128)(2,1)S(1)}, u32[]{:S(2)}, u32[]{:S(2)}) collective-permute-start(bf16[32,1024]{1,0:T(8,128)(2,1)S(1)} %collective-permute-done.10), channel_id=1, source_target_pairs={{0,2},{2,4},{4,6},{6,8},{8,10},{10,12},{12,14},{14,16},{16,18},{18... | collective-permute-start | bytes 196616 | tf_op jit(solution)/shard_map/ppermute | solution.py:22
  76.2 6.4 %collective-permute-start.13 = (bf16[32,1024]{1,0:T(8,128)(2,1)S(1)}, bf16[32,1024]{1,0:T(8,128)(2,1)S(1)}, u32[]{:S(2)}, u32[]{:S(2)}) collective-permute-start(bf16[32,1024]{1,0:T(8,128)(2,1)S(1)} %collective-permute-done.11), channel_id=1, source_target_pairs={{0,30},{2,0},{4,2},{6,4},{8,6},{10,8},{12,10},{14,12},{16,14},{18,... | collective-permute-start | bytes 196616 | tf_op jit(solution)/shard_map/ppermute | solution.py:27
  82.5 6.4 %collective-permute-start.14 = (bf16[32,1024]{1,0:T(8,128)(2,1)S(1)}, bf16[32,1024]{1,0:T(8,128)(2,1)S(1)}, u32[]{:S(2)}, u32[]{:S(2)}) collective-permute-start(bf16[32,1024]{1,0:T(8,128)(2,1)S(1)} %collective-permute-done.12), channel_id=1, source_target_pairs={{0,2},{2,4},{4,6},{6,8},{8,10},{10,12},{12,14},{14,16},{16,18},{18... | collective-permute-start | bytes 196616 | tf_op jit(solution)/shard_map/ppermute | solution.py:22
  226.7 4.3 %copy-start.2 = (f32[2048]{0:T(1024)S(1)}, f32[2048]{0:T(1024)}, u32[]{:S(2)}) copy-start(f32[2048]{0:T(1024)} %param.32) | copy-start | bytes 24580
  231.0 19.3 %copy-start.7 = (f32[1024]{0:T(1024)S(1)}, f32[1024]{0:T(1024)}, u32[]{:S(2)}) copy-start(f32[1024]{0:T(1024)} %param.34) | copy-start | bytes 12292
  231.0 19.3 %copy-start.8 = (f32[1024]{0:T(1024)S(1)}, f32[1024]{0:T(1024)}, u32[]{:S(2)}) copy-start(f32[1024]{0:T(1024)} %param.30) | copy-start | bytes 12292
  231.0 59.5 %copy-start.9 = (s32[512]{0:T(512)S(1)}, s32[512]{0:T(512)}, u32[]{:S(2)}) copy-start(s32[512]{0:T(512)} %param.40) | copy-start | bytes 6148
  241.1 49.5 %all-gather.2.cloned.1.call-start = ((), (), s32[]{:S(2)}) async-start(), calls=%async_computation.2 | async-start | bytes 1114112 | tf_op jit(solution)/shard_map/all_gather | solution.py:225
  (4 other events, 15.4 us)
Sparse Core Ops, SparseCore 0:
  241.2 9.1 reduce-scatter.1
  252.5 37.9 all-gather.1
